TPU v7x, 32 devices: a whole 2x2x4 slice. The times are simulated.
32 devices in a mesh: dp: 8 (over z, x), tensor: 4 (over y, core).
Axes of the slice: x: 2, y: 2, z: 4, core: 2. Of those that a mesh axis runs over, the one named last changes fastest.
Arguments:
- features: bfloat16 [3072, 8192], P('dp', 'tensor'), may hold values from -6 to 6
- key_value_weight: bfloat16 [8192, 2048], P('tensor'), may hold values from -0.0625 to 0.0625
- adapter_down_weight: bfloat16 [32, 64, 8192], P('dp', None, 'tensor'), may hold values from -0.0625 to 0.0625
- adapter_up_weight: bfloat16 [32, 64, 2048], P('dp', None, 'tensor'), may hold values from -0.75 to 0.75
- token_adapter_index: int32 [3072], P('dp'), may hold values from 0 to 31, as said below
- adapter_position: int32 [32], replicated, may hold values from 0 to 31, as said below
- output_gradient: bfloat16 [3072, 2048], P('dp', 'tensor'), may hold values from -6 to 6
Outputs:
- key_value_output: bfloat16 [3072, 2048], P('dp', 'tensor')
- feature_gradient: bfloat16 [3072, 8192], P('dp', 'tensor')
- down_gradient: float32 [32, 64, 8192], P('dp', None, 'tensor')
- up_gradient: float32 [32, 64, 2048], P('dp', None, 'tensor')
Inputs may be any that keep to these rules, and one draw needn't show every extreme that they name: `token_adapter_index`: within each aligned block of 384 tokens (those of one index of dp) the ids do not fall. Call slot // 4 the storing index of an adapter; in each block at most 144 tokens have adapters of one storing index. In every draw one storing index, the same for all blocks, gets exactly 144 tokens from every block, and in every block another storing index, which varies from block to block, gets exactly 144 tokens as well. A permutation: adapter a is stored at slot adapter_position[a].
All inputs are finite; a program needn't handle non-finite values.
Results may differ from a plain program's by a relative error of at most 0.0054.
Values may be sent and summed in bfloat16 or wider, within the bound.
A program may use at most 64 MiB of HBM per device.

v0:
```python
import jax
import jax.numpy as jnp
from jax import lax
from jax.sharding import PartitionSpec as P

adapter_scale = 2.0


def contract_trailing(left, right):
    return lax.dot_general(
        left, right, (((1,), (1,)), ((), ())), preferred_element_type=jnp.float32
    )


def contract_leading(left, right):
    return lax.dot_general(
        left, right, (((0,), (0,)), ((), ())), preferred_element_type=jnp.float32
    )


def body(
    features,
    key_value_weight,
    adapter_down_weight,
    adapter_up_weight,
    token_adapter_index,
    adapter_position,
    output_gradient,
):
    token_groups = lax.axis_size("dp")
    tok_rows, width_local = features.shape
    output_local = output_gradient.shape[1]
    adapter_local_count, rank_axis_size, unused_value = adapter_down_weight.shape
    row_capacity = 3 * tok_rows // token_groups
    holding_rows = token_groups * row_capacity
    adapter_ids = jnp.arange(adapter_position.shape[0], dtype=jnp.int32)
    matches = token_adapter_index[:, None] == adapter_ids[None, :]
    slot_tok = jnp.sum(jnp.where(matches, adapter_position[None, :], 0), axis=1)
    owner_of = slot_tok // adapter_local_count
    local_id = slot_tok % adapter_local_count
    owner_hits = (owner_of[:, None] == jnp.arange(token_groups, dtype=jnp.int32)[None, :]).astype(
        jnp.int32
    )
    rank_in = jnp.sum((jnp.cumsum(owner_hits, axis=0) - 1) * owner_hits, axis=1)
    target_slot = owner_of * row_capacity + rank_in

    def to_buffer(source):
        filled = (
            jnp.zeros((holding_rows, source.shape[1]), source.dtype).at[target_slot].set(source)
        )
        return filled.reshape(token_groups, row_capacity, source.shape[1])

    id_buffer = (
        jnp.full((holding_rows,), -1.0, jnp.bfloat16)
        .at[target_slot]
        .set(local_id.astype(jnp.bfloat16))
    )
    id_buffer = id_buffer.reshape(token_groups, row_capacity)
    lane_ids = (
        jnp.arange(adapter_local_count * rank_axis_size, dtype=jnp.int32) // rank_axis_size
    ).astype(jnp.bfloat16)
    down_matrix = adapter_down_weight.reshape(adapter_local_count * rank_axis_size, width_local)
    up_matrix = adapter_up_weight.reshape(adapter_local_count * rank_axis_size, output_local)

    def compact_rows(values, slot_selector):
        return jnp.sum(
            (values * slot_selector).reshape(holding_rows, adapter_local_count, rank_axis_size),
            axis=1,
        )

    def expand(values, slot_selector):
        return (
            jnp.tile(values, (1, adapter_local_count)).astype(jnp.float32) * slot_selector
        ).astype(jnp.bfloat16)

    columns = key_value_weight
    gradient_frozen = contract_trailing(
        lax.all_gather(output_gradient, "tensor", axis=1, tiled=True), columns
    )
    rows_recv, ids_recv = (
        lax.all_to_all(to_buffer(features), "dp", split_axis=0, concat_axis=0, tiled=True),
        lax.all_to_all(id_buffer, "dp", split_axis=0, concat_axis=0, tiled=True),
    )
    rows_in = rows_recv.reshape(holding_rows, width_local)
    slot_selector = (ids_recv.reshape(holding_rows)[:, None] == lane_ids[None, :]).astype(
        jnp.float32
    )
    down_part = compact_rows(contract_trailing(rows_in, down_matrix), slot_selector)
    down_total = lax.psum(down_part, "tensor")
    down_gathered = expand(down_total.astype(jnp.bfloat16), slot_selector)
    adapter_row_block = (
        adapter_scale * jnp.dot(down_gathered, up_matrix, preferred_element_type=jnp.float32)
    ).astype(jnp.bfloat16)
    adapter_backward = lax.all_to_all(
        adapter_row_block.reshape(token_groups, row_capacity, output_local),
        "dp",
        split_axis=0,
        concat_axis=0,
        tiled=True,
    )
    grads_recv = lax.all_to_all(
        to_buffer(output_gradient), "dp", split_axis=0, concat_axis=0, tiled=True
    )
    incoming_gradients = grads_recv.reshape(holding_rows, output_local)
    up_partial = compact_rows(
        adapter_scale * contract_trailing(incoming_gradients, up_matrix), slot_selector
    )
    up_combined = lax.psum(up_partial, "tensor")
    up_wide = expand(up_combined.astype(jnp.bfloat16), slot_selector)
    input_row_block = jnp.dot(up_wide, down_matrix, preferred_element_type=jnp.float32).astype(
        jnp.bfloat16
    )
    input_back = lax.all_to_all(
        input_row_block.reshape(token_groups, row_capacity, width_local),
        "dp",
        split_axis=0,
        concat_axis=0,
        tiled=True,
    )
    down_gradient = contract_leading(up_wide, rows_in).reshape(
        adapter_local_count, rank_axis_size, width_local
    )
    up_gradient = (adapter_scale * contract_leading(down_gathered, incoming_gradients)).reshape(
        adapter_local_count, rank_axis_size, output_local
    )
    adapter_token_rows = adapter_backward.reshape(holding_rows, output_local)[target_slot]
    input_tok = input_back.reshape(holding_rows, width_local)[target_slot]
    columns = key_value_weight
    key_value_frozen = lax.psum_scatter(
        contract_leading(columns, features.T), "tensor", scatter_dimension=0, tiled=True
    ).T
    key_value_output = (key_value_frozen + adapter_token_rows.astype(jnp.float32)).astype(
        jnp.bfloat16
    )
    feature_gradient = (gradient_frozen + input_tok.astype(jnp.float32)).astype(jnp.bfloat16)
    return (key_value_output, feature_gradient, down_gradient, up_gradient)


def solution(mesh):
    placed = (
        P("dp", "tensor"),
        P("tensor", None),
        P("dp", None, "tensor"),
        P("dp", None, "tensor"),
        P("dp"),
        P(),
        P("dp", "tensor"),
    )
    return jax.shard_map(
        body,
        mesh=mesh,
        in_specs=placed,
        out_specs=(
            P("dp", "tensor"),
            P("dp", "tensor"),
            P("dp", None, "tensor"),
            P("dp", None, "tensor"),
        ),
        check_vma=False,
    )
```

profile of v0, /device:TPU:0, one launch (start us, length us, event | category | flops | bytes accessed | tf_op | source)
XLA Modules:
  0.0 354.7 jit_solution(9046061355832921624)
XLA Ops:
  7.2 0.0 copy-start
  7.2 0.9 select_reduce_fusion
  8.1 0.9 reduce-window.6
  9.0 0.2 slice_reduce_fusion
  9.2 0.1 fusion.16
  9.4 3.0 scatter_custom_fusion
  12.3 0.7 all_to_all.24
  13.0 7.3 %all-to-all-start = ((bf16[8,1,144]{2,1,0:T(2,128)(2,1)}), bf16[8,1,144]{2,1,0:T(2,128)(2,1)S(1)}, u32[]{:S(2)}, u32[]{:S(2)}) async-start(bf16[8,1,144]{2,1,0:T(2,128)(2,1)} %all_to_all.24), calls=%async_computation.1 | async-start | bytes 16384 | tf_op jit(solution)/shard_map/all_to_all | solution.py:82
  20.3 3.6 %scatter_custom_fusion.2 = bf16[1152,512]{1,0:T(8,128)(2,1)} fusion(s32[384]{0:T(512)S(1)} %fusion.27, bf16[384,512]{1,0:T(8,128)(2,1)} %param.13, bf16[]{:T(256)} %constant.71.clone.1), kind=kCustom, calls=%fused_computation.25 | custom fusion | bytes 1180160 | tf_op jit(solution)/shard_map/scatter | solution.py:49
  23.9 3.0 all-to-all-done
  26.8 3.6 %all-to-all-start.3 = ((bf16[8,144,512]{2,1,0:T(8,128)(2,1)}), bf16[8,144,512]{2,1,0:T(8,128)(2,1)S(1)}, u32[]{:S(2)}, u32[]{:S(2)}) async-start(bf16[8,144,512]{2,1,0:T(8,128)(2,1)} %bitcast.11), calls=%async_computation.4 | async-start | bytes 2359296 | tf_op jit(solution)/shard_map/all_to_all | solution.py:101
  30.4 6.7 %scatter_custom_fusion.1 = bf16[1152,2048]{1,0:T(8,128)(2,1)} fusion(s32[384]{0:T(512)S(1)} %fusion.27, bf16[384,2048]{1,0:T(8,128)(2,1)} %param.7, bf16[]{:T(256)} %constant.71.clone.1), kind=kCustom, calls=%fused_computation.13 | custom fusion | bytes 4719104 | tf_op jit(solution)/shard_map/scatter | solution.py:49
  37.1 21.0 %all-to-all-done.3 = bf16[8,144,512]{2,1,0:T(8,128)(2,1)S(1)} async-done(((bf16[8,144,512]{2,1,0:T(8,128)(2,1)}), bf16[8,144,512]{2,1,0:T(8,128)(2,1)S(1)}, u32[]{:S(2)}, u32[]{:S(2)}) %all-to-all-start.3) | async-done | bytes 1179680 | tf_op jit(solution)/shard_map/all_to_all | solution.py:101
  58.1 4.8 %all-to-all-start.1 = ((bf16[8,144,2048]{2,1,0:T(8,128)(2,1)}), bf16[8,144,2048]{2,1,0:T(8,128)(2,1)}, u32[]{:S(2)}, u32[]{:S(2)}) async-start(bf16[8,144,2048]{2,1,0:T(8,128)(2,1)} %bitcast.74), calls=%async_computation.2 | async-start | bytes 9437184 | tf_op jit(solution)/shard_map/all_to_all | solution.py:81
  62.9 0.6 fusion.20
  63.5 0.1 eq.81
  63.6 0.0 copy-start.2
  63.6 1.5 fusion.2
  65.1 0.8 reduce_sum.48
  65.9 100.3 %all-to-all-done.1 = bf16[8,144,2048]{2,1,0:T(8,128)(2,1)} async-done(((bf16[8,144,2048]{2,1,0:T(8,128)(2,1)}), bf16[8,144,2048]{2,1,0:T(8,128)(2,1)}, u32[]{:S(2)}, u32[]{:S(2)}) %all-to-all-start.1) | async-done | bytes 4718624 | tf_op jit(solution)/shard_map/all_to_all | solution.py:81
  166.3 3.9 %convolution_select_fusion = f32[1152,256]{0,1:T(8,128)S(1)} fusion(bf16[1152,2048]{1,0:T(8,128)(2,1)} %bitcast.5, bf16[256,2048]{1,0:T(8,128)(2,1)S(1)} %bitcast.73, bf16[1152]{0:T(1024)(128)(2,1)S(1)} %eq.81, bf16[256]{0:T(256)(128)(2,1)S(1)} %fusion.28), kind=kOutput, calls=%fused_computation.12 | convolution fusion | flops 1208549376 | bytes 6949632 | tf_op jit(solution)/shard_map/dot_general | solution.py:10
  170.2 0.8 reduce_sum.47
  171.0 17.6 %all-reduce.2 = (bf16[1152,64]{0,1:T(8,128)(2,1)S(1)}, bf16[1152,64]{0,1:T(8,128)(2,1)S(1)}) all-reduce(f32[1152,64]{0,1:T(8,128)} %reduce_sum.47, f32[1152,64]{0,1:T(8,128)} %reduce_sum.48), channel_id=1, replica_groups=mesh['dp'=8,'tensor'=4] {'tensor'}, use_global_device_ids=true, to_apply=%region_8.9 | all-reduce | flops 147456 | bytes 884736 | tf_op jit(solution)/shard_map/psum | solution.py:89
  188.6 0.0 copy-start.1
  188.6 2.6 fusion.1
  191.2 4.0 %all-to-all-start.2 = ((bf16[8,144,512]{2,1,0:T(8,128)(2,1)}), bf16[8,144,512]{2,1,0:T(8,128)(2,1)S(1)}, u32[]{:S(2)}, u32[]{:S(2)}) async-start(bf16[8,144,512]{2,1,0:T(8,128)(2,1)} %bitcast.80), calls=%async_computation.3 | async-start | bytes 2359296 | tf_op jit(solution)/shard_map/all_to_all | solution.py:94
  195.3 0.0 reduce-scatter.2.cloned.1.call-start
  195.3 10.0 %fusion.31 = f32[2048,384]{1,0:T(8,128)} fusion(bf16[2048,2048]{1,0:T(8,128)(2,1)} %param.8, bf16[384,2048]{1,0:T(8,128)(2,1)} %param.7), kind=kOutput, calls=%fused_computation.79 | convolution fusion | flops 3221225472 | bytes 13107200 | tf_op jit(solution)/shard_map/dot_general | solution.py:16
  205.3 0.0 reduce-scatter.2.cloned.1.call-update
  205.3 4.4 %bitcast_convert_fusion = bf16[1152,2048]{1,0:T(8,128)(2,1)} fusion(bf16[4,64,2048]{2,1,0:T(8,128)(2,1)S(1)} %copy-done, bf16[1152,64]{0,1:T(8,128)(2,1)S(1)} %get-tuple-element.21, bf16[4,64]{1,0:T(4,128)(2,1)} %fusion.20, bf16[1152]{0:T(1024)(128)(2,1)} %copy-done.2), kind=kOutput, calls=%fused_computation.5 | convolution fusion | flops 1211498496 | bytes 5917440 | tf_op jit(solution)/shard_map/dot_general | solution.py:110
  209.8 13.9 %all-to-all-done.2 = bf16[8,144,512]{2,1,0:T(8,128)(2,1)S(1)} async-done(((bf16[8,144,512]{2,1,0:T(8,128)(2,1)}), bf16[8,144,512]{2,1,0:T(8,128)(2,1)S(1)}, u32[]{:S(2)}, u32[]{:S(2)}) %all-to-all-start.2) | async-done | bytes 1179680 | tf_op jit(solution)/shard_map/all_to_all | solution.py:94
  223.7 4.6 %all-to-all-start.4 = ((bf16[8,144,2048]{2,1,0:T(8,128)(2,1)}), bf16[8,144,2048]{2,1,0:T(8,128)(2,1)}, u32[]{:S(2)}, u32[]{:S(2)}) async-start(bf16[8,144,2048]{2,1,0:T(8,128)(2,1)} %bitcast.76), calls=%async_computation.5 | async-start | bytes 9437184 | tf_op jit(solution)/shard_map/all_to_all | solution.py:113
  228.3 0.3 all-gather.2.cloned.1.call-start
  228.6 0.5 all-gather.2.cloned.1.call-update
  229.1 1.3 pad_clamp_fusion
  230.4 0.9 fusion.7
  231.3 1.1 fusion.5
  232.4 1.3 convolution_multiply_fusion.1
  233.7 5.2 %fusion.32 = f32[4,64,2048]{2,1,0:T(8,128)} fusion(bf16[4,64,1152]{2,1,0:T(8,128)(2,1)S(1)} %bitcast.83, bf16[1152,2048,1]{1,0,2:T(8,128)(2,1)} %bitcast.21), kind=kOutput, calls=%fused_computation.80 | convolution fusion | flops 1207959552 | bytes 7405568 | tf_op jit(solution)/shard_map/dot_general | solution.py:16
  238.9 2.1 gather_fusion
  241.0 0.2 copy.19
  241.2 3.0 reduce-scatter.2.cloned.1.call-done
  244.2 1.2 fusion.8
  245.5 0.9 copy.20
  246.4 85.7 %all-to-all-done.4 = bf16[8,144,2048]{2,1,0:T(8,128)(2,1)} async-done(((bf16[8,144,2048]{2,1,0:T(8,128)(2,1)}), bf16[8,144,2048]{2,1,0:T(8,128)(2,1)}, u32[]{:S(2)}, u32[]{:S(2)}) %all-to-all-start.4) | async-done | bytes 4718624 | tf_op jit(solution)/shard_map/all_to_all | solution.py:113
  332.1 7.3 %gather_fusion.1 = bf16[384,2048]{1,0:T(8,128)(2,1)S(1)} fusion(bf16[1152,2048]{1,0:T(8,128)(2,1)} %bitcast.17, s32[1024]{0:T(1024)S(1)} %copy-done.3), kind=kCustom, calls=%fused_computation.1 | custom fusion | bytes 3147264 | tf_op jit(solution)/shard_map/gather | solution.py:127
  339.4 0.0 all-gather.2.cloned.1.call-done
  339.4 8.5 %add_convert_fusion = bf16[384,2048]{1,0:T(8,128)(2,1)} fusion(bf16[384,2048]{1,0:T(8,128)(2,1)S(1)} %gather_fusion.1, bf16[384,2048]{1,0:T(8,128)(2,1)} %all-gather.2.cloned.1.call-done, bf16[2048,2048]{1,0:T(8,128)(2,1)} %param.8), kind=kOutput, calls=%fused_computation.8 | convolution fusion | flops 3223584768 | bytes 13107200 | tf_op jit(solution)/shard_map/dot_general | solution.py:10
  (16 shorter events, 0.2 us)
Async XLA Ops:
  7.2 159.1 %copy-start = (bf16[4,64,2048]{2,1,0:T(8,128)(2,1)S(1)}, bf16[4,64,2048]{2,1,0:T(8,128)(2,1)}, u32[]{:S(2)}) copy-start(bf16[4,64,2048]{2,1,0:T(8,128)(2,1)} %param.9) | copy-start | bytes 3145732
  9.3 21.1 %copy-start.4 = (s32[384]{0:T(512)}, s32[384]{0:T(512)S(1)}, u32[]{:S(2)}) copy-start(s32[384]{0:T(512)S(1)} %fusion.27) | copy-start | bytes 4612
  13.0 13.8 %all-to-all-start = ((bf16[8,1,144]{2,1,0:T(2,128)(2,1)}), bf16[8,1,144]{2,1,0:T(2,128)(2,1)S(1)}, u32[]{:S(2)}, u32[]{:S(2)}) async-start(bf16[8,1,144]{2,1,0:T(2,128)(2,1)} %all_to_all.24), calls=%async_computation.1 | async-start | bytes 16384 | tf_op jit(solution)/shard_map/all_to_all | solution.py:82
  26.8 31.3 %all-to-all-start.3 = ((bf16[8,144,512]{2,1,0:T(8,128)(2,1)}), bf16[8,144,512]{2,1,0:T(8,128)(2,1)S(1)}, u32[]{:S(2)}, u32[]{:S(2)}) async-start(bf16[8,144,512]{2,1,0:T(8,128)(2,1)} %bitcast.11), calls=%async_computation.4 | async-start | bytes 2359296 | tf_op jit(solution)/shard_map/all_to_all | solution.py:101
  58.1 108.2 %all-to-all-start.1 = ((bf16[8,144,2048]{2,1,0:T(8,128)(2,1)}), bf16[8,144,2048]{2,1,0:T(8,128)(2,1)}, u32[]{:S(2)}, u32[]{:S(2)}) async-start(bf16[8,144,2048]{2,1,0:T(8,128)(2,1)} %bitcast.74), calls=%async_computation.2 | async-start | bytes 9437184 | tf_op jit(solution)/shard_map/all_to_all | solution.py:81
  62.9 103.4 %copy-start.5 = (bf16[256]{0:T(256)(128)(2,1)}, bf16[256]{0:T(256)(128)(2,1)S(1)}, u32[]{:S(2)}) copy-start(bf16[256]{0:T(256)(128)(2,1)S(1)} %fusion.28) | copy-start | bytes 1540
  63.6 102.7 %copy-start.2 = (bf16[1152]{0:T(1024)(128)(2,1)}, bf16[1152]{0:T(1024)(128)(2,1)S(1)}, u32[]{:S(2)}) copy-start(bf16[1152]{0:T(1024)(128)(2,1)S(1)} %eq.81) | copy-start | bytes 6916
  188.6 2.6 copy-start.1
  191.2 32.5 %all-to-all-start.2 = ((bf16[8,144,512]{2,1,0:T(8,128)(2,1)}), bf16[8,144,512]{2,1,0:T(8,128)(2,1)S(1)}, u32[]{:S(2)}, u32[]{:S(2)}) async-start(bf16[8,144,512]{2,1,0:T(8,128)(2,1)} %bitcast.80), calls=%async_computation.3 | async-start | bytes 2359296 | tf_op jit(solution)/shard_map/all_to_all | solution.py:94
  195.3 49.0 %reduce-scatter.2.cloned.1.call-start = ((), (), s32[]{:S(2)}) async-start(), calls=%async_computation.6 | async-start | bytes 3932160 | tf_op jit(solution)/shard_map/reduce_scatter | solution.py:129
  223.7 108.3 %all-to-all-start.4 = ((bf16[8,144,2048]{2,1,0:T(8,128)(2,1)}), bf16[8,144,2048]{2,1,0:T(8,128)(2,1)}, u32[]{:S(2)}, u32[]{:S(2)}) async-start(bf16[8,144,2048]{2,1,0:T(8,128)(2,1)} %bitcast.76), calls=%async_computation.5 | async-start | bytes 9437184 | tf_op jit(solution)/shard_map/all_to_all | solution.py:113
  228.3 111.1 %all-gather.2.cloned.1.call-start = ((), (), s32[]{:S(2)}) async-start(), calls=%async_computation.7 | async-start | bytes 1966080 | tf_op jit(solution)/shard_map/all_gather | solution.py:78
  233.7 5.3 %copy-start.3 = (s32[1024]{0:T(1024)S(1)}, s32[1024]{0:T(1024)}, u32[]{:S(2)}) copy-start(s32[1024]{0:T(1024)} %pad_clamp_fusion) | copy-start | bytes 12292
Sparse Core Ops, SparseCore 0:
  205.5 38.7 reduce-scatter.1
  245.8 19.6 all-gather.1
where the time goes:
time: 356 us; the launch traced here: 355 us
  waiting for transfers between devices  227 us (64%)
  matrix products  37.5 us (11%)
  local copies, waits for them, and re-layouts  24.8 us (7%)
  starting transfers between devices  24.6 us (7%)
  blocking collectives  17.6 us (5%)
  between operations  14.2 us (4%)
  other arithmetic  8.58 us (2%)
    all_to_all x1, waiting for transfers between devices, body(): lax.all_to_all(to_buffer(features), 'dp', split_axis=0, concat_axis=0, ti...  100 us
    all_to_all x1, waiting for transfers between devices, body(): lax.all_to_all(input_row_block.reshape(token_groups, row_capacity, width_...  85.7 us
    all_to_all x1, waiting for transfers between devices, body(): lax.all_to_all(to_buffer(output_gradient), 'dp', split_axis=0, concat_axi...  21 us
    psum x1, blocking collectives, body(): down_total = lax.psum(down_part, 'tensor')  17.6 us
    dot_general x3, matrix products, contract_leading(): lax.dot_general(left, right, (((0,), (0,)), ((), ())), preferred_element_...  16.6 us
    all_to_all x1, waiting for transfers between devices, body(): lax.all_to_all(adapter_row_block.reshape(token_groups, row_capacity, outp...  13.9 us
    dot_general x3, matrix products, contract_trailing(): lax.dot_general(left, right, (((1,), (1,)), ((), ())), preferred_element_...  13.8 us
    scatter x2, local copies, waits for them, and re-layouts, to_buffer(): jnp.zeros((holding_rows, source.shape[1]), source.dtype).at[target_slot]  10.3 us
  transfers between devices with their start and end apart: 7, of which 6 were waited for; matrix products, arithmetic and copies ran while one was open for 14% of the time, Pallas kernels for 0%

commit v1 on v0

--- a/solution.py
+++ b/solution.py
@@ -4,6 +4,30 @@
 from jax.sharding import PartitionSpec as P
 
 adapter_scale = 2.0
+
+
+def in_blocks(array, dim, count):
+    lengths = array.shape
+    tiles = array.reshape(*lengths[:dim], count, lengths[dim] // count, *lengths[dim + 1 :])
+    return jnp.moveaxis(tiles, dim, 0)
+
+
+def joined_along(blocks, dim):
+    blocks = jnp.moveaxis(blocks, 0, dim)
+    dims = blocks.shape
+    return blocks.reshape(*dims[:dim], dims[dim] * dims[dim + 1], *dims[dim + 2 :])
+
+
+def exchange_directly(x, axis, split_dim, concat_dim):
+    length, mine = (lax.axis_size(axis), lax.axis_index(axis))
+    blocks = in_blocks(x, split_dim, length)
+    out = blocks
+    for step in range(1, length):
+        target, source = ((mine + step) % length, (mine - step) % length)
+        sent = lax.dynamic_index_in_dim(blocks, target, 0)
+        other = lax.ppermute(sent, axis, [(i, (i + step) % length) for i in range(length)])
+        out = lax.dynamic_update_slice_in_dim(out, other, source, axis=0)
+    return joined_along(out, concat_dim)
 
 
 def contract_trailing(left, right):
@@ -91,12 +115,8 @@
     adapter_row_block = (
         adapter_scale * jnp.dot(down_gathered, up_matrix, preferred_element_type=jnp.float32)
     ).astype(jnp.bfloat16)
-    adapter_backward = lax.all_to_all(
-        adapter_row_block.reshape(token_groups, row_capacity, output_local),
-        "dp",
-        split_axis=0,
-        concat_axis=0,
-        tiled=True,
+    adapter_backward = exchange_directly(
+        adapter_row_block.reshape(token_groups, row_capacity, output_local), "dp", 0, 0
     )
     grads_recv = lax.all_to_all(
         to_buffer(output_gradient), "dp", split_axis=0, concat_axis=0, tiled=True

time: 356 us -> 360 us (1.011)
  starting transfers between devices: 24.6 us -> 54.2 us
  waiting for transfers between devices: 227 us -> 204 us
    ppermute x0 -> x7, waiting for transfers between devices: none -> 89.5 us  [exchange_directly(): lax.ppermute(sent, axis, [(i, (i + step) % length) for i in range(length)])]
    all_to_all x1, waiting for transfers between devices: 85.7 us -> 0.01 us  [body(): lax.all_to_all(input_row_block.reshape(token_groups, row_capacity, width_...]
    ppermute x0 -> x7, starting transfers between devices: none -> 33.8 us  [exchange_directly(): lax.ppermute(sent, axis, [(i, (i + step) % length) for i in range(length)])]
    all_to_all x1 -> x0, waiting for transfers between devices: 13.9 us -> none  [body(): lax.all_to_all(adapter_row_block.reshape(token_groups, row_capacity, outp...]
    all_to_all x1, waiting for transfers between devices: 100 us -> 90.2 us  [body(): lax.all_to_all(to_buffer(features), 'dp', split_axis=0, concat_axis=0, ti...]
    all_to_all x1 -> x0, starting transfers between devices: 4.04 us -> none  [body(): lax.all_to_all(adapter_row_block.reshape(token_groups, row_capacity, outp...]
  transfers between devices with their start and end apart: 7 -> 13, of which waited for: 6 -> 7; matrix products, arithmetic and copies ran while one was open for 14% -> 15% of each run, Pallas kernels for 0% -> 0%
where the time goes in v1:
time: 360 us; the launch traced here: 359 us
  waiting for transfers between devices  204 us (57%)
  starting transfers between devices  54.2 us (15%)
  matrix products  36.5 us (10%)
  local copies, waits for them, and re-layouts  25 us (7%)
  blocking collectives  18.1 us (5%)
  between operations  14.6 us (4%)
  other arithmetic  6.29 us (2%)
    all_to_all x1, waiting for transfers between devices, body(): lax.all_to_all(to_buffer(features), 'dp', split_axis=0, concat_axis=0, ti...  90.2 us
    ppermute x7, waiting for transfers between devices, exchange_directly(): lax.ppermute(sent, axis, [(i, (i + step) % length) for i in range(length)])  89.5 us
    ppermute x7, starting transfers between devices, exchange_directly(): lax.ppermute(sent, axis, [(i, (i + step) % length) for i in range(length)])  33.8 us
    all_to_all x1, waiting for transfers between devices, body(): lax.all_to_all(to_buffer(output_gradient), 'dp', split_axis=0, concat_axi...  21 us
    psum x1, blocking collectives, body(): down_total = lax.psum(down_part, 'tensor')  18.1 us
    dot_general x3, matrix products, contract_leading(): lax.dot_general(left, right, (((0,), (0,)), ((), ())), preferred_element_...  16.5 us
    dot_general x3, matrix products, contract_trailing(): lax.dot_general(left, right, (((1,), (1,)), ((), ())), preferred_element_...  13.8 us
    scatter x2, local copies, waits for them, and re-layouts, to_buffer(): jnp.zeros((holding_rows, source.shape[1]), source.dtype).at[target_slot]  10.3 us
  transfers between devices with their start and end apart: 13, of which 7 were waited for; matrix products, arithmetic and copies ran while one was open for 15% of the time, Pallas kernels for 0%

profile of v1, /device:TPU:0, one launch (start us, length us, event | category | flops | bytes accessed | tf_op | source)
XLA Modules:
  0.0 359.1 jit_solution(17974815096960726965)
XLA Ops:
  7.2 0.9 select_reduce_fusion
  8.1 0.9 reduce-window.6
  9.0 0.2 slice_reduce_fusion
  9.2 0.1 fusion.16
  9.4 3.0 scatter_custom_fusion
  12.3 0.7 all_to_all.20
  13.0 7.3 %all-to-all-start = ((bf16[8,1,144]{2,1,0:T(2,128)(2,1)}), bf16[8,1,144]{2,1,0:T(2,128)(2,1)S(1)}, u32[]{:S(2)}, u32[]{:S(2)}) async-start(bf16[8,1,144]{2,1,0:T(2,128)(2,1)} %all_to_all.20), calls=%async_computation.1 | async-start | bytes 16384 | tf_op jit(solution)/shard_map/all_to_all | solution.py:106
  20.3 3.6 scatter_custom_fusion.2
  23.9 3.0 all-to-all-done
  26.8 3.6 all-to-all-start.2
  30.4 6.7 %scatter_custom_fusion.1 = bf16[1152,2048]{1,0:T(8,128)(2,1)} fusion(s32[384]{0:T(512)S(1)} %fusion.27, bf16[384,2048]{1,0:T(8,128)(2,1)} %param.7, bf16[]{:T(256)} %constant.166.clone.1), kind=kCustom, calls=%fused_computation.13 | custom fusion | bytes 4719104 | tf_op jit(solution)/shard_map/scatter | solution.py:73
  37.1 21.0 %all-to-all-done.2 = bf16[8,144,512]{2,1,0:T(8,128)(2,1)S(1)} async-done(((bf16[8,144,512]{2,1,0:T(8,128)(2,1)}), bf16[8,144,512]{2,1,0:T(8,128)(2,1)S(1)}, u32[]{:S(2)}, u32[]{:S(2)}) %all-to-all-start.2) | async-done | bytes 1179680 | tf_op jit(solution)/shard_map/all_to_all | solution.py:121
  58.1 4.6 %all-to-all-start.1 = ((bf16[8,144,2048]{2,1,0:T(8,128)(2,1)}), bf16[8,144,2048]{2,1,0:T(8,128)(2,1)}, u32[]{:S(2)}, u32[]{:S(2)}) async-start(bf16[8,144,2048]{2,1,0:T(8,128)(2,1)} %bitcast.74), calls=%async_computation.2 | async-start | bytes 9437184 | tf_op jit(solution)/shard_map/all_to_all | solution.py:105
  62.7 0.2 reduce-scatter.2.cloned.1.call-start
  62.9 10.0 %fusion.31 = f32[2048,384]{1,0:T(8,128)} fusion(bf16[2048,2048]{1,0:T(8,128)(2,1)} %param.8, bf16[384,2048]{1,0:T(8,128)(2,1)} %param.7), kind=kOutput, calls=%fused_computation.93 | convolution fusion | flops 3221225472 | bytes 13107200 | tf_op jit(solution)/shard_map/dot_general | solution.py:40
  73.0 0.6 fusion.20
  73.6 0.1 eq.96
  73.7 1.5 fusion.2
  75.2 0.8 reduce_sum.48
  76.0 90.2 %all-to-all-done.1 = bf16[8,144,2048]{2,1,0:T(8,128)(2,1)} async-done(((bf16[8,144,2048]{2,1,0:T(8,128)(2,1)}), bf16[8,144,2048]{2,1,0:T(8,128)(2,1)}, u32[]{:S(2)}, u32[]{:S(2)}) %all-to-all-start.1) | async-done | bytes 4718624 | tf_op jit(solution)/shard_map/all_to_all | solution.py:105
  166.2 3.9 %convolution_select_fusion = f32[1152,256]{0,1:T(8,128)S(1)} fusion(bf16[1152,2048]{1,0:T(8,128)(2,1)} %bitcast.5, bf16[256,2048]{1,0:T(8,128)(2,1)S(1)} %bitcast.73, bf16[1152]{0:T(1024)(128)(2,1)S(1)} %eq.96, bf16[256]{0:T(256)(128)(2,1)S(1)} %fusion.28), kind=kOutput, calls=%fused_computation.12 | convolution fusion | flops 1208549376 | bytes 6949632 | tf_op jit(solution)/shard_map/dot_general | solution.py:34
  170.1 0.8 reduce_sum.47
  170.9 18.1 %all-reduce.2 = (bf16[1152,64]{0,1:T(8,128)(2,1)}, bf16[1152,64]{0,1:T(8,128)(2,1)S(1)}) all-reduce(f32[1152,64]{0,1:T(8,128)} %reduce_sum.47, f32[1152,64]{0,1:T(8,128)} %reduce_sum.48), channel_id=1, replica_groups=mesh['dp'=8,'tensor'=4] {'tensor'}, use_global_device_ids=true, to_apply=%region_8.9 | all-reduce | flops 147456 | bytes 884736 | tf_op jit(solution)/shard_map/psum | solution.py:113
  188.9 4.4 %bitcast_convert_fusion = bf16[1152,2048]{1,0:T(8,128)(2,1)} fusion(bf16[4,64,2048]{2,1,0:T(8,128)(2,1)S(1)} %copy-done, bf16[1152,64]{0,1:T(8,128)(2,1)S(1)} %get-tuple-element.21, bf16[4,64]{1,0:T(4,128)(2,1)} %fusion.20, bf16[1152]{0:T(1024)(128)(2,1)} %copy-done.2), kind=kOutput, calls=%fused_computation.5 | convolution fusion | flops 1211498496 | bytes 5917440 | tf_op jit(solution)/shard_map/dot_general | solution.py:130
  193.4 4.7 %all-to-all-start.3 = ((bf16[8,144,2048]{2,1,0:T(8,128)(2,1)}), bf16[8,144,2048]{2,1,0:T(8,128)(2,1)}, u32[]{:S(2)}, u32[]{:S(2)}) async-start(bf16[8,144,2048]{2,1,0:T(8,128)(2,1)} %bitcast.78), calls=%async_computation.4 | async-start | bytes 9437184 | tf_op jit(solution)/shard_map/all_to_all | solution.py:133
  198.1 0.0 all-gather.2.cloned.1.call-start
  198.2 0.7 all-gather.2.cloned.1.call-update
  199.1 0.6 pad_clamp_fusion
  199.8 1.7 fusion.1
  201.5 0.2 fusion.7
  201.7 1.9 collective-permute-start
  203.6 0.2 fusion.5
  203.8 5.2 %fusion.32 = f32[4,64,2048]{2,1,0:T(8,128)} fusion(bf16[4,64,1152]{2,1,0:T(8,128)(2,1)S(1)} %bitcast.84, bf16[1152,2048,1]{1,0,2:T(8,128)(2,1)} %bitcast.21), kind=kOutput, calls=%fused_computation.94 | convolution fusion | flops 1207959552 | bytes 7405568 | tf_op jit(solution)/shard_map/dot_general | solution.py:40
  209.0 73.6 %collective-permute-done = bf16[1,1,144,512]{3,2,0,1:T(8,128)(2,1)S(1)} collective-permute-done((bf16[1,1,144,512]{3,2,0,1:T(8,128)(2,1)S(1)}, bf16[1,1,144,512]{3,2,0,1:T(8,128)(2,1)S(1)}, u32[]{:S(2)}, u32[]{:S(2)}) %collective-permute-start) | collective-permute-done | bytes 147488 | tf_op jit(solution)/shard_map/ppermute | solution.py:28
  282.6 0.1 constant_dynamic-slice_fusion
  282.7 22.9 %collective-permute-start.2 = (bf16[1,1,144,512]{3,2,0,1:T(8,128)(2,1)S(1)}, bf16[1,1,144,512]{3,2,0,1:T(8,128)(2,1)S(1)}, u32[]{:S(2)}, u32[]{:S(2)}) collective-permute-start(bf16[1,1,144,512]{3,2,0,1:T(8,128)(2,1)S(1)} %get-tuple-element.26), channel_id=1, source_target_pairs={{0,12},{4,16},{8,20},{12,24},{16,28},{20,0},{24,4},{28,8},{1,13},{... | collective-permute-start | bytes 442376 | tf_op jit(solution)/shard_map/ppermute | solution.py:28
  305.6 1.3 convolution_multiply_fusion.1
  306.9 6.6 %collective-permute-start.6 = (bf16[1,1,144,512]{3,2,0,1:T(8,128)(2,1)S(1)}, bf16[1,1,144,512]{3,2,0,1:T(8,128)(2,1)S(1)}, u32[]{:S(2)}, u32[]{:S(2)}) collective-permute-start(bf16[1,1,144,512]{3,2,0,1:T(8,128)(2,1)S(1)} %get-tuple-element.22), channel_id=1, source_target_pairs={{0,28},{4,0},{8,4},{12,8},{16,12},{20,16},{24,20},{28,24},{1,29},{... | collective-permute-start | bytes 442376 | tf_op jit(solution)/shard_map/ppermute | solution.py:28
  313.5 0.6 collective-permute-done.1
  314.1 2.3 collective-permute-start.3
  316.5 0.6 collective-permute-done.2
  317.1 14.8 %collective-permute-done.3 = bf16[1,1,144,512]{3,2,0,1:T(8,128)(2,1)S(1)} collective-permute-done((bf16[1,1,144,512]{3,2,0,1:T(8,128)(2,1)S(1)}, bf16[1,1,144,512]{3,2,0,1:T(8,128)(2,1)S(1)}, u32[]{:S(2)}, u32[]{:S(2)}) %collective-permute-start.3) | collective-permute-done | bytes 147488 | tf_op jit(solution)/shard_map/ppermute | solution.py:28
  331.9 2.1 gather_fusion
  334.0 0.2 copy.19
  334.3 1.2 fusion.8
  335.5 0.9 copy.20
  336.4 7.3 %gather_fusion.1 = bf16[384,2048]{1,0:T(8,128)(2,1)S(1)} fusion(bf16[1152,2048]{1,0:T(8,128)(2,1)} %bitcast.17, s32[1024]{0:T(1024)S(1)} %copy-done.4), kind=kCustom, calls=%fused_computation.1 | custom fusion | bytes 3147264 | tf_op jit(solution)/shard_map/gather | solution.py:147
  343.8 8.5 %add_convert_fusion = bf16[384,2048]{1,0:T(8,128)(2,1)} fusion(bf16[384,2048]{1,0:T(8,128)(2,1)S(1)} %gather_fusion.1, bf16[384,2048]{1,0:T(8,128)(2,1)} %all-gather.2.cloned.1.call-done, bf16[2048,2048]{1,0:T(8,128)(2,1)} %param.8), kind=kOutput, calls=%fused_computation.8 | convolution fusion | flops 3223584768 | bytes 13107200 | tf_op jit(solution)/shard_map/dot_general | solution.py:34
  (44 shorter events, 0.4 us)
Async XLA Ops:
  7.2 159.0 %copy-start = (bf16[4,64,2048]{2,1,0:T(8,128)(2,1)S(1)}, bf16[4,64,2048]{2,1,0:T(8,128)(2,1)}, u32[]{:S(2)}) copy-start(bf16[4,64,2048]{2,1,0:T(8,128)(2,1)} %param.9) | copy-start | bytes 3145732
  9.3 21.1 %copy-start.5 = (s32[384]{0:T(512)}, s32[384]{0:T(512)S(1)}, u32[]{:S(2)}) copy-start(s32[384]{0:T(512)S(1)} %fusion.27) | copy-start | bytes 4612
  13.0 13.8 %all-to-all-start = ((bf16[8,1,144]{2,1,0:T(2,128)(2,1)}), bf16[8,1,144]{2,1,0:T(2,128)(2,1)S(1)}, u32[]{:S(2)}, u32[]{:S(2)}) async-start(bf16[8,1,144]{2,1,0:T(2,128)(2,1)} %all_to_all.20), calls=%async_computation.1 | async-start | bytes 16384 | tf_op jit(solution)/shard_map/all_to_all | solution.py:106
  26.8 31.3 %all-to-all-start.2 = ((bf16[8,144,512]{2,1,0:T(8,128)(2,1)}), bf16[8,144,512]{2,1,0:T(8,128)(2,1)S(1)}, u32[]{:S(2)}, u32[]{:S(2)}) async-start(bf16[8,144,512]{2,1,0:T(8,128)(2,1)} %bitcast.11), calls=%async_computation.3 | async-start | bytes 2359296 | tf_op jit(solution)/shard_map/all_to_all | solution.py:121
  58.1 108.1 %all-to-all-start.1 = ((bf16[8,144,2048]{2,1,0:T(8,128)(2,1)}), bf16[8,144,2048]{2,1,0:T(8,128)(2,1)}, u32[]{:S(2)}, u32[]{:S(2)}) async-start(bf16[8,144,2048]{2,1,0:T(8,128)(2,1)} %bitcast.74), calls=%async_computation.2 | async-start | bytes 9437184 | tf_op jit(solution)/shard_map/all_to_all | solution.py:105
  62.7 271.6 %reduce-scatter.2.cloned.1.call-start = ((), (), s32[]{:S(2)}) async-start(), calls=%async_computation.5 | async-start | bytes 3932160 | tf_op jit(solution)/shard_map/reduce_scatter | solution.py:149
  73.0 93.2 %copy-start.8 = (bf16[256]{0:T(256)(128)(2,1)}, bf16[256]{0:T(256)(128)(2,1)S(1)}, u32[]{:S(2)}) copy-start(bf16[256]{0:T(256)(128)(2,1)S(1)} %fusion.28) | copy-start | bytes 1540
  73.7 92.5 %copy-start.2 = (bf16[1152]{0:T(1024)(128)(2,1)}, bf16[1152]{0:T(1024)(128)(2,1)S(1)}, u32[]{:S(2)}) copy-start(bf16[1152]{0:T(1024)(128)(2,1)S(1)} %eq.96) | copy-start | bytes 6916
  193.4 5.8 %copy-start.6 = (s32[384]{0:T(512)S(1)}, s32[384]{0:T(512)}, u32[]{:S(2)}) copy-start(s32[384]{0:T(512)} %copy-done.5) | copy-start | bytes 4612
  193.4 143.0 %all-to-all-start.3 = ((bf16[8,144,2048]{2,1,0:T(8,128)(2,1)}), bf16[8,144,2048]{2,1,0:T(8,128)(2,1)}, u32[]{:S(2)}, u32[]{:S(2)}) async-start(bf16[8,144,2048]{2,1,0:T(8,128)(2,1)} %bitcast.78), calls=%async_computation.4 | async-start | bytes 9437184 | tf_op jit(solution)/shard_map/all_to_all | solution.py:133
  198.1 145.6 %all-gather.2.cloned.1.call-start = ((), (), s32[]{:S(2)}) async-start(), calls=%async_computation.6 | async-start | bytes 1966080 | tf_op jit(solution)/shard_map/all_gather | solution.py:102
  199.7 1.7 copy-start.3
  199.7 1.7 copy-start.9
  199.7 3.8 %copy-start.1 = (bf16[1152,64]{0,1:T(8,128)(2,1)S(1)}, bf16[1152,64]{0,1:T(8,128)(2,1)}, u32[]{:S(2)}) copy-start(bf16[1152,64]{0,1:T(8,128)(2,1)} %get-tuple-element.20) | copy-start | bytes 442372
  199.8 3.8 %copy-start.7 = (bf16[4,64]{1,0:T(4,128)(2,1)S(1)}, bf16[4,64]{1,0:T(4,128)(2,1)}, u32[]{:S(2)}) copy-start(bf16[4,64]{1,0:T(4,128)(2,1)} %fusion.20) | copy-start | bytes 1540
  201.7 80.9 %collective-permute-start = (bf16[1,1,144,512]{3,2,0,1:T(8,128)(2,1)S(1)}, bf16[1,1,144,512]{3,2,0,1:T(8,128)(2,1)S(1)}, u32[]{:S(2)}, u32[]{:S(2)}) collective-permute-start(bf16[1,1,144,512]{3,2,0,1:T(8,128)(2,1)S(1)} %constant_dynamic-slice_fusion.6), channel_id=1, source_target_pairs={{0,4},{4,8},{8,12},{12,16},{16,20},{20,24},{24,28},{28,0},{1,5},{5... | collective-permute-start | bytes 442376 | tf_op jit(solution)/shard_map/ppermute | solution.py:28
  282.7 34.4 %collective-permute-start.2 = (bf16[1,1,144,512]{3,2,0,1:T(8,128)(2,1)S(1)}, bf16[1,1,144,512]{3,2,0,1:T(8,128)(2,1)S(1)}, u32[]{:S(2)}, u32[]{:S(2)}) collective-permute-start(bf16[1,1,144,512]{3,2,0,1:T(8,128)(2,1)S(1)} %get-tuple-element.26), channel_id=1, source_target_pairs={{0,12},{4,16},{8,20},{12,24},{16,28},{20,0},{24,4},{28,8},{1,13},{... | collective-permute-start | bytes 442376 | tf_op jit(solution)/shard_map/ppermute | solution.py:28
  305.6 8.6 %collective-permute-start.1 = (bf16[1,1,144,512]{3,2,0,1:T(8,128)(2,1)S(1)}, bf16[1,1,144,512]{3,2,0,1:T(8,128)(2,1)S(1)}, u32[]{:S(2)}, u32[]{:S(2)}) collective-permute-start(bf16[1,1,144,512]{3,2,0,1:T(8,128)(2,1)S(1)} %get-tuple-element.27), channel_id=1, source_target_pairs={{0,8},{4,12},{8,16},{12,20},{16,24},{20,28},{24,0},{28,4},{1,9},{5... | collective-permute-start | bytes 442376 | tf_op jit(solution)/shard_map/ppermute | solution.py:28
  306.9 25.1 %copy-start.4 = (s32[1024]{0:T(1024)S(1)}, s32[1024]{0:T(1024)}, u32[]{:S(2)}) copy-start(s32[1024]{0:T(1024)} %pad_clamp_fusion) | copy-start | bytes 12292
  306.9 25.0 %collective-permute-start.6 = (bf16[1,1,144,512]{3,2,0,1:T(8,128)(2,1)S(1)}, bf16[1,1,144,512]{3,2,0,1:T(8,128)(2,1)S(1)}, u32[]{:S(2)}, u32[]{:S(2)}) collective-permute-start(bf16[1,1,144,512]{3,2,0,1:T(8,128)(2,1)S(1)} %get-tuple-element.22), channel_id=1, source_target_pairs={{0,28},{4,0},{8,4},{12,8},{16,12},{20,16},{24,20},{28,24},{1,29},{... | collective-permute-start | bytes 442376 | tf_op jit(solution)/shard_map/ppermute | solution.py:28
  313.5 18.3 %collective-permute-start.5 = (bf16[1,1,144,512]{3,2,0,1:T(8,128)(2,1)S(1)}, bf16[1,1,144,512]{3,2,0,1:T(8,128)(2,1)S(1)}, u32[]{:S(2)}, u32[]{:S(2)}) collective-permute-start(bf16[1,1,144,512]{3,2,0,1:T(8,128)(2,1)S(1)} %get-tuple-element.23), channel_id=1, source_target_pairs={{0,24},{4,28},{8,0},{12,4},{16,8},{20,12},{24,16},{28,20},{1,25},{... | collective-permute-start | bytes 442376 | tf_op jit(solution)/shard_map/ppermute | solution.py:28
  313.5 18.3 %collective-permute-start.4 = (bf16[1,1,144,512]{3,2,0,1:T(8,128)(2,1)S(1)}, bf16[1,1,144,512]{3,2,0,1:T(8,128)(2,1)S(1)}, u32[]{:S(2)}, u32[]{:S(2)}) collective-permute-start(bf16[1,1,144,512]{3,2,0,1:T(8,128)(2,1)S(1)} %get-tuple-element.24), channel_id=1, source_target_pairs={{0,20},{4,24},{8,28},{12,0},{16,4},{20,8},{24,12},{28,16},{1,21},{... | collective-permute-start | bytes 442376 | tf_op jit(solution)/shard_map/ppermute | solution.py:28
  314.1 17.7 %collective-permute-start.3 = (bf16[1,1,144,512]{3,2,0,1:T(8,128)(2,1)S(1)}, bf16[1,1,144,512]{3,2,0,1:T(8,128)(2,1)S(1)}, u32[]{:S(2)}, u32[]{:S(2)}) collective-permute-start(bf16[1,1,144,512]{3,2,0,1:T(8,128)(2,1)S(1)} %get-tuple-element.25), channel_id=1, source_target_pairs={{0,16},{4,20},{8,24},{12,28},{16,0},{20,4},{24,8},{28,12},{1,17},{... | collective-permute-start | bytes 442376 | tf_op jit(solution)/shard_map/ppermute | solution.py:28
Sparse Core Ops, SparseCore 0:
  73.1 38.9 reduce-scatter.1
  200.5 20.5 all-gather.1
